TPU v7x, 512 devices: a whole 4x8x8 slice. The times are simulated.
512 devices in a mesh: stu: 16 (over z_lo, x), que: 32 (over z_hi, y, core).
Axes of the slice: x: 4, y: 8, z: 8 (z_hi: 2, z_lo: 4; z = z_hi * 4 + z_lo), core: 2. Of those that a mesh axis runs over, the one named last changes fastest.
Arguments:
- codes: int32 [4096, 4096], P('stu', 'que'), may hold values from 0 to 2
- theta: float32 [4096, 64], P(('stu', 'que')), may hold values from -6 to 6
- disc: float32 [4096, 64], P(('que', 'stu')), may hold values from -0.75 to 0.75
- intercept: float32 [4096], P(('que', 'stu')), may hold values from -5 to 5
Outputs:
- step_abilities: float32 [4096, 64], P(('stu', 'que'))
- step_disc: float32 [4096, 64], P(('que', 'stu'))
- step_intercept: float32 [4096], P(('que', 'stu'))
All inputs are finite; a program needn't handle non-finite values.
Results may differ from a plain program's by a relative error of at most 0.0003.
Values sent between devices are 32-bit elements; how exact they have to be, the bound alone decides.
A program may use at most 64 MiB of HBM per device.

v0:
```python
import jax
import jax.numpy as jnp
from jax import lax
from jax.sharding import PartitionSpec as P

ITERS = 2
HIGH = lax.Precision.HIGHEST


def matmul(left, right):
    return jnp.dot(left, right, precision=HIGH, preferred_element_type=jnp.float32)


def contract_rows(left, right):
    return lax.dot_general(
        left, right, (((0,), (0,)), ((), ())), precision=HIGH, preferred_element_type=jnp.float32
    )


def local_inner(left, right):
    return jnp.sum(left[0] * right[0]) + jnp.sum(left[1] * right[1]) + jnp.sum(left[2] * right[2])


def squared(residual, precond):
    return lax.psum(local_inner(residual, precond), ("stu", "que"))


def combine(first, factor, second):
    return jax.tree.map(lambda u, v: u + factor * v, first, second)


def shards(codes, theta, disc, intercept):
    theta_rows = lax.all_gather(theta, "que", axis=0, tiled=True)
    disc_cols, icpt_cols = (
        lax.all_gather(disc, "stu", axis=0, tiled=True),
        lax.all_gather(intercept, "stu", axis=0, tiled=True),
    )
    logit = matmul(theta_rows, disc_cols.T) + icpt_cols[None, :]
    prob = jax.nn.sigmoid(logit)
    observed = (codes > 0).astype(jnp.float32)
    correct = (codes == 2).astype(jnp.float32)
    resid = observed * (prob - correct)
    weight = observed * prob * (1.0 - prob)
    row_one = matmul(resid, disc_cols)
    row_two = matmul(weight, disc_cols * disc_cols)
    col_one = contract_rows(resid, theta_rows)
    col_two = contract_rows(weight, theta_rows * theta_rows)
    col_three = jnp.sum(resid, 0)
    col_four = jnp.sum(weight, 0)
    row_sum = (
        lax.psum_scatter(row_one, "que", scatter_dimension=0, tiled=True),
        lax.psum_scatter(row_two, "que", scatter_dimension=0, tiled=True),
    )
    col_sum = (
        lax.psum_scatter(col_one, "stu", scatter_dimension=0, tiled=True),
        lax.psum_scatter(col_two, "stu", scatter_dimension=0, tiled=True),
        lax.psum_scatter(col_three, "stu", scatter_dimension=0, tiled=True),
        lax.psum_scatter(col_four, "stu", scatter_dimension=0, tiled=True),
    )
    own = (theta, disc, intercept)
    grad = (row_sum[0] + own[0], col_sum[0] + own[1], col_sum[2] + own[2])
    diag = (row_sum[1] + 1.0, col_sum[1] + 1.0, col_sum[3] + 1.0)
    solution = jax.tree.map(jnp.zeros_like, grad)
    residual = jax.tree.map(lambda u: -u, grad)
    precond = jax.tree.map(lambda u, d: u / d, residual, diag)
    direction = precond
    norm_now = squared(residual, precond)
    for step in range(ITERS):
        vt_rows = lax.all_gather(direction[0], "que", axis=0, tiled=True)
        va_cols = lax.all_gather(direction[1], "stu", axis=0, tiled=True)
        vb_cols = lax.all_gather(direction[2], "stu", axis=0, tiled=True)
        left = jnp.concatenate([vt_rows, theta_rows], 1)
        right = jnp.concatenate([disc_cols, va_cols], 1)
        change = matmul(left, right.T) + vb_cols[None, :]
        scaled = weight * change
        part_rows = matmul(scaled, disc_cols)
        part_disc = contract_rows(scaled, theta_rows)
        part_icpt = jnp.sum(scaled, 0)
        summed_rows = lax.psum_scatter(part_rows, "que", scatter_dimension=0, tiled=True)
        summed_disc = lax.psum_scatter(part_disc, "stu", scatter_dimension=0, tiled=True)
        summed_icpt = lax.psum_scatter(part_icpt, "stu", scatter_dimension=0, tiled=True)
        image = (summed_rows + direction[0], summed_disc + direction[1], summed_icpt + direction[2])
        alpha = norm_now / lax.psum(local_inner(direction, image), ("stu", "que"))
        solution = combine(solution, alpha, direction)
        residual = combine(residual, -alpha, image)
        if step + 1 < ITERS:
            precond = jax.tree.map(lambda u, d: u / d, residual, diag)
            norm_next = squared(residual, precond)
            ratio = norm_next / norm_now
            direction = combine(precond, ratio, direction)
            norm_now = norm_next
    result = jax.tree.map(lambda u, d: u * jnp.sqrt(d), solution, diag)
    return (result[0], result[1], result[2])


def solution(mesh):
    placed = (P("stu", "que"), P(("stu", "que"), None), P(("que", "stu"), None), P(("que", "stu")))
    return jax.shard_map(
        shards,
        mesh=mesh,
        in_specs=placed,
        out_specs=(P(("stu", "que"), None), P(("que", "stu"), None), P(("que", "stu"))),
        check_vma=False,
    )
```

profile of v0, /device:TPU:1, one launch (start us, length us, event | category | flops | bytes accessed | tf_op | source)
XLA Modules:
  0.0 1810.6 jit_solution(3583325412611648461)
XLA Ops:
  7.2 60.0 %all_gather.27 = f32[256,64]{1,0:T(8,128)S(1)} all-gather(f32[8,64]{1,0:T(8,128)} %param.5), channel_id=1, replica_groups=mesh['stu'=16,'que'=32] {'que'}, dimensions={0}, use_global_device_ids=true | all-gather | bytes 67584 | tf_op jit(solution)/shard_map/all_gather | solution.py:33
  69.4 36.2 %all-reduce = f32[128]{0:T(128)S(1)} all-reduce(f32[128]{0:T(128)S(1)} %dynamic-update-slice), channel_id=1, replica_groups=mesh['stu'=16,'que'=32] {'stu'}, use_global_device_ids=true, to_apply=%add | all-reduce | flops 128 | bytes 1024
  105.6 30.4 %all_gather.28 = f32[128,64]{1,0:T(8,128)S(1)} all-gather(f32[8,64]{1,0:T(8,128)S(1)} %copy-done.1), channel_id=1, replica_groups=mesh['stu'=16,'que'=32] {'stu'}, dimensions={0}, use_global_device_ids=true | all-gather | bytes 34816 | tf_op jit(solution)/shard_map/all_gather | solution.py:35
  136.4 1.0 fusion.37
  137.4 1.0 fusion.10
  138.4 32.3 %all-reduce.20 = (f32[128]{0:T(128)S(1)}, f32[128]{0:T(128)S(1)}) all-reduce(f32[128]{0:T(128)S(1)} %get-tuple-element.35, f32[128]{0:T(128)S(1)} %get-tuple-element.31), channel_id=6, replica_groups=mesh['stu'=16,'que'=32] {'stu'}, use_global_device_ids=true, to_apply=%region_7.0.clone | all-reduce | flops 256 | bytes 2048
  172.1 0.9 fusion.38
  173.0 0.9 fusion.18
  174.0 1.3 dynamic-slice.3
  176.0 152.3 %all-reduce.32.cloned.1.call-done = (f32[128,64]{1,0:T(8,128)}, f32[128,64]{1,0:T(8,128)}, f32[128]{0:T(128)}) async-done(((f32[128,64]{1,0:T(8,128)}, f32[128,64]{1,0:T(8,128)}, f32[128]{0:T(128)}), (f32[128,64]{1,0:T(8,128)}, f32[128,64]{1,0:T(8,128)}, f32[128]{0:T(128)})) %all-reduce.32.cloned.1.call-update) | async-done | bytes 66064
  328.9 35.5 %all_gather.31 = f32[128,64]{1,0:T(8,128)S(1)} all-gather(f32[8,64]{1,0:T(8,128)S(1)} %get-tuple-element.26), channel_id=1, replica_groups=mesh['stu'=16,'que'=32] {'stu'}, dimensions={0}, use_global_device_ids=true | all-gather | bytes 34816 | tf_op jit(solution)/shard_map/all_gather | solution.py:70
  364.4 318.1 %all-reduce.30.cloned.1.call-done = (f32[256,64]{1,0:T(8,128)}, f32[256,64]{1,0:T(8,128)}) async-done(((f32[256,64]{1,0:T(8,128)}, f32[256,64]{1,0:T(8,128)}), (f32[256,64]{1,0:T(8,128)}, f32[256,64]{1,0:T(8,128)})) %all-reduce.30.cloned.1.call-update) | async-done | bytes 131088
  683.2 47.3 %all_gather.30 = f32[256,64]{1,0:T(8,128)S(1)} all-gather(f32[8,64]{1,0:T(8,128)S(1)} %get-tuple-element.33), channel_id=1, replica_groups=mesh['stu'=16,'que'=32] {'que'}, dimensions={0}, use_global_device_ids=true | all-gather | bytes 67584 | tf_op jit(solution)/shard_map/all_gather | solution.py:69
  731.6 0.9 fusion.50
  733.0 67.3 %all-reduce.18 = (f32[128,64]{1,0:T(8,128)S(1)}, f32[128]{0:T(128)S(1)}) all-reduce(f32[128,64]{1,0:T(8,128)S(1)} %fusion.51, f32[128]{0:T(128)S(1)} %get-tuple-element.39), channel_id=9, replica_groups=mesh['stu'=16,'que'=32] {'stu'}, use_global_device_ids=true, to_apply=%region_14.0.clone | all-reduce | flops 8320 | bytes 66560
  800.9 0.8 multiply_reduce_fusion.7
  801.7 247.6 %all-reduce.26.cloned.1.call-done = f32[256,64]{1,0:T(8,128)} async-done(((f32[256,64]{1,0:T(8,128)}), f32[256,64]{1,0:T(8,128)}) %all-reduce.26.cloned.1.call-update) | async-done | bytes 65552
  1049.3 1.3 multiply_reduce_fusion.3
  1054.4 98.3 %all-reduce.15 = (f32[]{:T(128)}, f32[]{:T(128)}) all-reduce(f32[]{:T(128)S(6)} %add.156, f32[]{:T(128)S(6)} %add.163), channel_id=1, replica_groups=mesh['stu'=16,'que'=32] {'stu','que'}, use_global_device_ids=true, to_apply=%region_11.0 | all-reduce | flops 2 | bytes 16 | tf_op jit(solution)/shard_map/psum | solution.py:25
  1154.1 1.4 multiply_reduce_fusion
  1156.1 1.3 multiply_reduce_fusion.1
  1159.3 94.4 %psum.30 = f32[]{:T(128)} all-reduce(f32[]{:T(128)S(6)} %add.168), channel_id=1, replica_groups=mesh['stu'=16,'que'=32] {'stu','que'}, use_global_device_ids=true, to_apply=%region_23.0 | all-reduce | flops 1 | bytes 8 | tf_op jit(solution)/shard_map/psum | solution.py:25
  1255.8 34.9 %all-reduce.2 = f32[128]{0:T(128)S(1)} all-reduce(f32[128]{0:T(128)S(1)} %get-tuple-element.22), channel_id=1, replica_groups=mesh['stu'=16,'que'=32] {'stu'}, use_global_device_ids=true, to_apply=%add.2 | all-reduce | flops 128 | bytes 1024
  1290.8 30.4 %all_gather.34 = f32[128,64]{1,0:T(8,128)S(1)} all-gather(f32[8,64]{1,0:T(8,128)S(1)} %multiply_add_fusion), channel_id=1, replica_groups=mesh['stu'=16,'que'=32] {'stu'}, dimensions={0}, use_global_device_ids=true | all-gather | bytes 34816 | tf_op jit(solution)/shard_map/all_gather | solution.py:70
  1321.9 63.4 %all_gather.33 = f32[256,64]{1,0:T(8,128)S(1)} all-gather(f32[8,64]{1,0:T(8,128)S(1)} %multiply_add_fusion.1), channel_id=1, replica_groups=mesh['stu'=16,'que'=32] {'que'}, dimensions={0}, use_global_device_ids=true | all-gather | bytes 67584 | tf_op jit(solution)/shard_map/all_gather | solution.py:69
  1385.6 0.9 fusion.52
  1387.0 64.5 %all-reduce.17 = (f32[128,64]{1,0:T(8,128)S(1)}, f32[128]{0:T(128)S(1)}) all-reduce(f32[128,64]{1,0:T(8,128)S(1)} %fusion.53, f32[128]{0:T(128)S(1)} %get-tuple-element.41), channel_id=12, replica_groups=mesh['stu'=16,'que'=32] {'stu'}, use_global_device_ids=true, to_apply=%region_26.0.clone | all-reduce | flops 8320 | bytes 66560
  1452.1 0.7 fusion.30
  1452.8 246.5 %all-reduce.28.cloned.1.call-done = f32[256,64]{1,0:T(8,128)} async-done(((f32[256,64]{1,0:T(8,128)}), f32[256,64]{1,0:T(8,128)}) %all-reduce.28.cloned.1.call-update) | async-done | bytes 65552
  1699.3 1.3 fusion.22
  1702.5 98.3 %psum.31 = f32[]{:T(128)} all-reduce(f32[]{:T(128)S(6)} %add.178), channel_id=1, replica_groups=mesh['stu'=16,'que'=32] {'stu','que'}, use_global_device_ids=true, to_apply=%region_31.0 | all-reduce | flops 1 | bytes 8 | tf_op jit(solution)/shard_map/psum | solution.py:83
  1802.2 1.3 sqrt_multiply_fusion
  (42 shorter events, 10.4 us)
Async XLA Ops:
  7.2 128.9 %copy-start = (s32[256,128]{1,0:T(8,128)S(1)}, s32[256,128]{1,0:T(8,128)}, u32[]{:S(2)}) copy-start(s32[256,128]{1,0:T(8,128)} %param.4) | copy-start | bytes 393220
  7.2 321.0 %all-reduce.32.cloned.1.call-start = ((), (), s32[]{:S(2)}) async-start(), calls=%async_computation.3 | async-start | bytes 263168
  67.2 0.7 copy-start.5
  68.5 0.7 copy-start.6
  69.2 36.4 %copy-start.1 = (f32[8,64]{1,0:T(8,128)S(1)}, f32[8,64]{1,0:T(8,128)}, u32[]{:S(2)}) copy-start(f32[8,64]{1,0:T(8,128)} %param.6) | copy-start | bytes 6148
  171.5 0.5 copy-start.4
  172.1 510.4 %all-reduce.30.cloned.1.call-start = ((), (), s32[]{:S(2)}) async-start(), calls=%async_computation.2 | async-start | bytes 524288
  174.0 875.3 %all-reduce.26.cloned.1.call-start = ((), (), s32[]{:S(2)}) async-start(), calls=%async_computation | async-start | bytes 262144
  328.9 353.6 %copy-start.2 = (f32[8,64]{1,0:T(8,128)S(1)}, f32[8,64]{1,0:T(8,128)}, u32[]{:S(2)}) copy-start(f32[8,64]{1,0:T(8,128)} %param.5) | copy-start | bytes 6148
  730.5 0.7 copy-start.3
  732.9 966.4 %all-reduce.28.cloned.1.call-start = ((), (), s32[]{:S(2)}) async-start(), calls=%async_computation.1 | async-start | bytes 262144
Sparse Core Ops, SparseCore 0:
  172.2 155.9 all-reduce.31
  331.1 351.3 all-reduce.29
  733.0 316.2 all-reduce.25
  1387.1 312.2 all-reduce.27
where the time goes:
time: 1810 us
  waiting for transfers between devices  965 us (53%)
  blocking collectives  793 us (44%)
  between operations  27.5 us (2%)
    unnamed x8, waiting for transfers between devices  965 us
    unnamed x5, blocking collectives  235 us
    psum x2, blocking collectives, squared(): return lax.psum(local_inner(residual, precond), ('stu', 'que'))  193 us
    all_gather x2, blocking collectives, shards(): vt_rows = lax.all_gather(direction[0], 'que', axis=0, tiled=True)  111 us
    psum x1, blocking collectives, shards(): alpha = norm_now / lax.psum(local_inner(direction, image), ('stu', 'que'))  98.3 us
    all_gather x2, blocking collectives, shards(): va_cols = lax.all_gather(direction[1], 'stu', axis=0, tiled=True)  65.9 us
    all_gather x1, blocking collectives, shards(): theta_rows = lax.all_gather(theta, 'que', axis=0, tiled=True)  60 us
  transfers between devices with their start and end apart: 4, of which 4 were waited for; matrix products, arithmetic and copies ran while one was open for 0% of the time, Pallas kernels for 0%

commit v1 on v0

--- a/solution.py
+++ b/solution.py
@@ -66,7 +66,9 @@
     direction = precond
     norm_now = squared(residual, precond)
     for step in range(ITERS):
-        vt_rows = lax.all_gather(direction[0], "que", axis=0, tiled=True)
+        vt_rows = jnp.concatenate(
+            lax.all_to_all(jnp.stack([direction[0]] * lax.axis_size("que")), "que", 0, 0), axis=0
+        )
         va_cols = lax.all_gather(direction[1], "stu", axis=0, tiled=True)
         vb_cols = lax.all_gather(direction[2], "stu", axis=0, tiled=True)
         left = jnp.concatenate([vt_rows, theta_rows], 1)

time: 1810 us -> 1740 us (0.961)
  blocking collectives: 793 us -> 675 us
  starting transfers between devices: 0.16 us -> 18.9 us
    all_gather x2 -> x0, blocking collectives: 111 us -> none  [shards(): vt_rows = lax.all_gather(direction[0], 'que', axis=0, tiled=True)]
    unnamed x8, waiting for transfers between devices: 965 us -> 983 us
    all_to_all x0 -> x2, starting transfers between devices: none -> 18.7 us  [shards(): lax.all_to_all(jnp.stack([direction[0]] * lax.axis_size('que')), 'que', 0...]
  transfers between devices with their start and end apart: 4 -> 6, of which waited for: 4 -> 4; matrix products, arithmetic and copies ran while one was open for 0% -> 0% of each run, Pallas kernels for 0% -> 0%
where the time goes in v1:
time: 1740 us; the launch traced here: 1730 us
  waiting for transfers between devices  983 us (56%)
  blocking collectives  675 us (39%)
  between operations  27.4 us (2%)
  starting transfers between devices  18.9 us (1%)
    unnamed x8, waiting for transfers between devices  983 us
    unnamed x5, blocking collectives  229 us
    psum x2, blocking collectives, squared(): return lax.psum(local_inner(residual, precond), ('stu', 'que'))  193 us
    psum x1, blocking collectives, shards(): alpha = norm_now / lax.psum(local_inner(direction, image), ('stu', 'que'))  98.3 us
    all_gather x2, blocking collectives, shards(): va_cols = lax.all_gather(direction[1], 'stu', axis=0, tiled=True)  65.1 us
    all_gather x1, blocking collectives, shards(): theta_rows = lax.all_gather(theta, 'que', axis=0, tiled=True)  60 us
  transfers between devices with their start and end apart: 6, of which 4 were waited for; matrix products, arithmetic and copies ran while one was open for 0% of the time, Pallas kernels for 0%

profile of v1, /device:TPU:1, one launch (start us, length us, event | category | flops | bytes accessed | tf_op | source)
XLA Modules:
  0.0 1734.0 jit_solution(1418670617363818204)
XLA Ops:
  7.2 60.0 %all_gather.21 = f32[256,64]{1,0:T(8,128)S(1)} all-gather(f32[8,64]{1,0:T(8,128)} %param.5), channel_id=1, replica_groups=mesh['stu'=16,'que'=32] {'que'}, dimensions={0}, use_global_device_ids=true | all-gather | bytes 67584 | tf_op jit(solution)/shard_map/all_gather | solution.py:33
  69.4 36.2 %all-reduce = f32[128]{0:T(128)S(1)} all-reduce(f32[128]{0:T(128)S(1)} %dynamic-update-slice), channel_id=1, replica_groups=mesh['stu'=16,'que'=32] {'stu'}, use_global_device_ids=true, to_apply=%add | all-reduce | flops 128 | bytes 1024
  105.6 30.4 %all_gather.22 = f32[128,64]{1,0:T(8,128)S(1)} all-gather(f32[8,64]{1,0:T(8,128)S(1)} %copy-done.2), channel_id=1, replica_groups=mesh['stu'=16,'que'=32] {'stu'}, dimensions={0}, use_global_device_ids=true | all-gather | bytes 34816 | tf_op jit(solution)/shard_map/all_gather | solution.py:35
  136.4 0.9 fusion.38
  137.3 0.9 fusion.18
  138.3 1.0 fusion.37
  139.3 1.0 fusion.10
  140.3 32.7 %all-reduce.20 = (f32[128]{0:T(128)S(1)}, f32[128]{0:T(128)S(1)}) all-reduce(f32[128]{0:T(128)S(1)} %get-tuple-element.35, f32[128]{0:T(128)S(1)} %get-tuple-element.31), channel_id=6, replica_groups=mesh['stu'=16,'que'=32] {'stu'}, use_global_device_ids=true, to_apply=%region_7.0.clone | all-reduce | flops 256 | bytes 2048
  174.4 1.3 dynamic-slice.3
  176.3 308.9 %all-reduce.30.cloned.1.call-done = (f32[256,64]{1,0:T(8,128)}, f32[256,64]{1,0:T(8,128)}) async-done(((f32[256,64]{1,0:T(8,128)}, f32[256,64]{1,0:T(8,128)}), (f32[256,64]{1,0:T(8,128)}, f32[256,64]{1,0:T(8,128)})) %all-reduce.30.cloned.1.call-update) | async-done | bytes 131088
  486.7 9.8 all-to-all-start
  496.6 137.9 %all-reduce.32.cloned.1.call-done = (f32[128,64]{1,0:T(8,128)}, f32[128,64]{1,0:T(8,128)}, f32[128]{0:T(128)}) async-done(((f32[128,64]{1,0:T(8,128)}, f32[128,64]{1,0:T(8,128)}, f32[128]{0:T(128)}), (f32[128,64]{1,0:T(8,128)}, f32[128,64]{1,0:T(8,128)}, f32[128]{0:T(128)})) %all-reduce.32.cloned.1.call-update) | async-done | bytes 66064
  635.1 35.0 %all_gather.24 = f32[128,64]{1,0:T(8,128)S(1)} all-gather(f32[8,64]{1,0:T(8,128)S(1)} %get-tuple-element.26), channel_id=1, replica_groups=mesh['stu'=16,'que'=32] {'stu'}, dimensions={0}, use_global_device_ids=true | all-gather | bytes 34816 | tf_op jit(solution)/shard_map/all_gather | solution.py:72
  670.7 0.8 reduce
  672.6 0.9 fusion.50
  673.9 62.3 %all-reduce.18 = (f32[128,64]{1,0:T(8,128)S(1)}, f32[128]{0:T(128)S(1)}) all-reduce(f32[128,64]{1,0:T(8,128)S(1)} %fusion.51, f32[128]{0:T(128)S(1)} %get-tuple-element.39), channel_id=9, replica_groups=mesh['stu'=16,'que'=32] {'stu'}, use_global_device_ids=true, to_apply=%region_14.0.clone | all-reduce | flops 8320 | bytes 66560
  737.6 268.9 %all-reduce.26.cloned.1.call-done = f32[256,64]{1,0:T(8,128)} async-done(((f32[256,64]{1,0:T(8,128)}), f32[256,64]{1,0:T(8,128)}) %all-reduce.26.cloned.1.call-update) | async-done | bytes 65552
  1006.4 1.4 multiply_reduce_fusion.3
  1011.6 98.3 %all-reduce.15 = (f32[]{:T(128)}, f32[]{:T(128)}) all-reduce(f32[]{:T(128)S(6)} %add.156, f32[]{:T(128)S(6)} %add.163), channel_id=1, replica_groups=mesh['stu'=16,'que'=32] {'stu','que'}, use_global_device_ids=true, to_apply=%region_11.0 | all-reduce | flops 2 | bytes 16 | tf_op jit(solution)/shard_map/psum | solution.py:25
  1111.2 1.3 multiply_reduce_fusion
  1113.3 1.3 multiply_reduce_fusion.1
  1116.4 94.4 %psum.30 = f32[]{:T(128)} all-reduce(f32[]{:T(128)S(6)} %add.168), channel_id=1, replica_groups=mesh['stu'=16,'que'=32] {'stu','que'}, use_global_device_ids=true, to_apply=%region_23.0 | all-reduce | flops 1 | bytes 8 | tf_op jit(solution)/shard_map/psum | solution.py:25
  1214.2 8.9 all-to-all-start.1
  1223.3 33.4 %all-reduce.2 = f32[128]{0:T(128)S(1)} all-reduce(f32[128]{0:T(128)S(1)} %get-tuple-element.22), channel_id=1, replica_groups=mesh['stu'=16,'que'=32] {'stu'}, use_global_device_ids=true, to_apply=%add.2 | all-reduce | flops 128 | bytes 1024
  1256.7 30.1 %all_gather.26 = f32[128,64]{1,0:T(8,128)S(1)} all-gather(f32[8,64]{1,0:T(8,128)S(1)} %multiply_add_fusion), channel_id=1, replica_groups=mesh['stu'=16,'que'=32] {'stu'}, dimensions={0}, use_global_device_ids=true | all-gather | bytes 34816 | tf_op jit(solution)/shard_map/all_gather | solution.py:72
  1286.8 0.8 reduce.1
  1288.1 0.9 fusion.52
  1289.4 64.4 %all-reduce.17 = (f32[128,64]{1,0:T(8,128)S(1)}, f32[128]{0:T(128)S(1)}) all-reduce(f32[128,64]{1,0:T(8,128)S(1)} %fusion.53, f32[128]{0:T(128)S(1)} %get-tuple-element.41), channel_id=12, replica_groups=mesh['stu'=16,'que'=32] {'stu'}, use_global_device_ids=true, to_apply=%region_26.0.clone | all-reduce | flops 8320 | bytes 66560
  1355.1 267.6 %all-reduce.28.cloned.1.call-done = f32[256,64]{1,0:T(8,128)} async-done(((f32[256,64]{1,0:T(8,128)}), f32[256,64]{1,0:T(8,128)}) %all-reduce.28.cloned.1.call-update) | async-done | bytes 65552
  1622.7 1.3 fusion.22
  1625.9 98.3 %psum.31 = f32[]{:T(128)} all-reduce(f32[]{:T(128)S(6)} %add.178), channel_id=1, replica_groups=mesh['stu'=16,'que'=32] {'stu','que'}, use_global_device_ids=true, to_apply=%region_31.0 | all-reduce | flops 1 | bytes 8 | tf_op jit(solution)/shard_map/psum | solution.py:85
  1725.5 1.3 sqrt_multiply_fusion
  (53 shorter events, 14.0 us)
Async XLA Ops:
  7.2 128.9 %copy-start = (s32[256,128]{1,0:T(8,128)S(1)}, s32[256,128]{1,0:T(8,128)}, u32[]{:S(2)}) copy-start(s32[256,128]{1,0:T(8,128)} %param.4) | copy-start | bytes 393220
  7.2 478.1 %all-reduce.30.cloned.1.call-start = ((), (), s32[]{:S(2)}) async-start(), calls=%async_computation.4 | async-start | bytes 524288
  67.2 0.7 copy-start.5
  68.5 0.7 copy-start.6
  69.2 36.4 %copy-start.2 = (f32[8,64]{1,0:T(8,128)S(1)}, f32[8,64]{1,0:T(8,128)}, u32[]{:S(2)}) copy-start(f32[8,64]{1,0:T(8,128)} %param.6) | copy-start | bytes 6148
  138.2 496.2 %all-reduce.32.cloned.1.call-start = ((), (), s32[]{:S(2)}) async-start(), calls=%async_computation.5 | async-start | bytes 263168
  173.8 0.5 copy-start.4
  175.7 309.6 %copy-start.1 = (f32[8,64]{1,0:T(8,128)S(1)}, f32[8,64]{1,0:T(8,128)}, u32[]{:S(2)}) copy-start(f32[8,64]{1,0:T(8,128)} %param.5) | copy-start | bytes 6148
  486.7 183.4 %all-to-all-start = ((f32[32,1,512]{2,1,0:T(1,128)}), f32[32,1,512]{2,1,0:T(1,128)S(1)}, u32[]{:S(2)}, u32[]{:S(2)}) async-start(f32[32,1,512]{2,1,0:T(1,128)} %reshape.48), calls=%async_computation | async-start | bytes 131072 | tf_op jit(solution)/shard_map/all_to_all | solution.py:70
  496.5 509.9 %all-reduce.26.cloned.1.call-start = ((), (), s32[]{:S(2)}) async-start(), calls=%async_computation.2 | async-start | bytes 262144
  671.5 0.7 copy-start.3
  1214.2 72.6 %all-to-all-start.1 = ((f32[32,1,512]{2,1,0:T(1,128)}), f32[32,1,512]{2,1,0:T(1,128)S(1)}, u32[]{:S(2)}, u32[]{:S(2)}) async-start(f32[32,1,512]{2,1,0:T(1,128)} %reshape.50), calls=%async_computation.1 | async-start | bytes 131072 | tf_op jit(solution)/shard_map/all_to_all | solution.py:70
  1223.1 399.5 %all-reduce.28.cloned.1.call-start = ((), (), s32[]{:S(2)}) async-start(), calls=%async_computation.3 | async-start | bytes 262144
Sparse Core Ops, SparseCore 0:
  138.4 346.8 all-reduce.29
  488.9 145.4 all-reduce.31
  674.0 332.3 all-reduce.25
  1289.5 333.1 all-reduce.27
